TPU v7x, 32 devices: a whole 2x2x4 slice. The times are simulated.
32 devices in a mesh: dp: 4 (over y, core), ctx: 8 (over z, x).
Axes of the slice: x: 2, y: 2, z: 4, core: 2. Of those that a mesh axis runs over, the one named last changes fastest.
Arguments:
- features: bfloat16 [4, 8, 248, 12288], P('dp', 'ctx'), may hold values from -6 to 6
- counts: int32 [4, 8], P('dp', 'ctx'), may hold values from 8 to 248, as said below
- short_taps: float32 [7, 3, 4096], P(None, None, 'ctx'), may hold values from -2 to 2
- residue: float32 [16, 256], P(None, 'ctx'), may hold values from -0.25 to 0.25
- decay_rate: float32 [16, 256], P(None, 'ctx'), may hold values from 1.953125e-05 to 0.05
- skip_gain: float32 [4096], P('ctx'), may hold values from -4 to 4
- cotangent: bfloat16 [4, 8, 248, 4096], P('dp', 'ctx'), may hold values from -6 to 6
Outputs:
- output: bfloat16 [4, 8, 248, 4096], P('dp', 'ctx')
- grad_features: bfloat16 [4, 8, 248, 12288], P('dp', 'ctx')
- grad_taps: float32 [7, 3, 4096], P(None, None, 'ctx')
- grad_residue: float32 [16, 256], P(None, 'ctx')
- grad_skip: float32 [4096], P('ctx')
Inputs may be any that keep to these rules, and one draw needn't show every extreme that they name: Along ctx the loader shards come in pairs 2m, 2m + 1 whose counts sum to 256; each replica has a shard holding exactly 248 rows; the counts of a replica sum to 1024.
All inputs are finite; a program needn't handle non-finite values.
Results may differ from a plain program's by a relative error of at most 0.0069.
Values may be sent and summed in bfloat16 or wider, within the bound.
A program may use at most 128 MiB of HBM per device.

v0:
```python
import jax
import jax.numpy as jnp
from jax import lax
from jax.sharding import PartitionSpec as P

TAPS = 7
TOK_DEV = 128


def modal_local(mixed, d_long, residue, decay_rate, row_block):
    highest = lax.Precision.HIGHEST
    length, channels = mixed.shape
    groups = residue.shape[1]
    group_size = channels // groups
    block_count = length // row_block
    lag_steps = jnp.arange(row_block, dtype=jnp.float32)
    decay_col = decay_rate[:, :, None]
    lag_powers = jnp.exp(-decay_col * lag_steps)
    kernel_rows = jnp.sum(residue[:, :, None] * lag_powers, axis=0)
    lag_int = jnp.arange(row_block, dtype=jnp.int32)
    lag_grid = lag_int[:, None] - lag_int[None, :]
    lower_part = lag_grid >= 0
    toeplitz = jnp.where(
        lower_part[None], jnp.take(kernel_rows, jnp.clip(lag_grid, 0, row_block - 1), axis=1), 0.0
    )
    out_powers = jnp.exp(-decay_col * (lag_steps + 1.0))
    in_powers = jnp.exp(-decay_col * (row_block - 1.0 - lag_steps))
    res_out = residue[:, :, None] * out_powers
    block_ids = jnp.arange(block_count, dtype=jnp.float32)
    block_gap = block_ids[:, None] - 1.0 - block_ids[None, :]
    carry_decay = jnp.where(
        block_gap >= 0.0,
        jnp.exp(-decay_rate[:, :, None, None] * row_block * jnp.maximum(block_gap, 0.0)),
        0.0,
    )
    lag_float = jnp.maximum(lag_grid, 0).astype(jnp.float32)
    mixed_blocks = mixed.reshape(block_count, row_block, groups, group_size)
    grad_blocks = d_long.reshape(block_count, row_block, groups, group_size)
    intra = jnp.einsum("gab,nbgq->nagq", toeplitz, mixed_blocks, precision=highest)
    local_state = jnp.einsum("rgb,nbgq->nrgq", in_powers, mixed_blocks, precision=highest)
    cross_state = jnp.einsum("rgij,jrgq->irgq", carry_decay, local_state, precision=highest)
    cross = jnp.einsum("rga,irgq->iagq", res_out, cross_state, precision=highest)
    long_part = (intra + cross).reshape(length, channels)
    du_intra = jnp.einsum("gab,nagq->nbgq", toeplitz, grad_blocks, precision=highest)
    d_cross = jnp.einsum("rga,iagq->irgq", res_out, grad_blocks, precision=highest)
    d_local = jnp.einsum("rgij,irgq->jrgq", carry_decay, d_cross, precision=highest)
    du_cross = jnp.einsum("rgb,nrgq->nbgq", in_powers, d_local, precision=highest)
    mixed_part = (du_intra + du_cross).reshape(length, channels)
    pair_sums = jnp.einsum("nagq,nbgq->gab", grad_blocks, mixed_blocks, precision=highest)

    def one_pole(pole_rates):
        weight = jnp.where(
            lower_part[None], jnp.exp(-pole_rates[:, None, None] * lag_float[None]), 0.0
        )
        return jnp.sum(pair_sums * weight, axis=(1, 2))

    grad_res = lax.map(one_pole, decay_rate)
    grad_res = grad_res + jnp.einsum(
        "iagq,rga,irgq->rg", grad_blocks, out_powers, cross_state, precision=highest
    )
    return (long_part, mixed_part, grad_res)


def moved_operator(features, counts, short_taps, residue, decay_rate, skip_gain, cotangent):
    shards = lax.axis_size("ctx")
    capacity = features.shape[2]
    model_width = cotangent.shape[3]
    channels = short_taps.shape[2]
    window_len = TOK_DEV * shards
    loader_in = features[0, 0].reshape(capacity, 3, model_width)
    cot_rows = cotangent[0, 0].reshape(capacity, 1, model_width)
    slot_ids = jnp.arange(capacity, dtype=jnp.int32)
    all_counts = lax.all_gather(counts, "ctx", axis=1, tiled=True)[0]
    shard_ends = jnp.cumsum(all_counts)
    shard_starts = shard_ends - all_counts
    positions = jnp.arange(window_len, dtype=jnp.int32)
    passed = shard_ends[None, :] <= positions[:, None]
    shard_of = jnp.sum(passed.astype(jnp.int32), axis=1)
    before = jnp.sum(jnp.where(passed, all_counts[None, :], 0), axis=1)
    take_index = shard_of * capacity + positions - before
    back_index = jnp.clip(shard_starts[:, None] + slot_ids[None, :], 0, window_len - 1).reshape(-1)
    back_valid = (slot_ids[None, :] < all_counts[:, None]).reshape(-1)

    def place(received):
        return jnp.take(received, take_index, axis=0)

    def inbound(loader_rows):
        return place(lax.all_to_all(loader_rows, "ctx", split_axis=2, concat_axis=0, tiled=True))

    def outbound(chan_rows):
        picked = jnp.take(chan_rows, back_index, axis=0)
        picked = jnp.where(back_valid[:, None, None], picked, jnp.zeros_like(picked))
        return lax.all_to_all(picked, "ctx", split_axis=0, concat_axis=2, tiled=True)

    window = inbound(loader_in)
    grad_chan = inbound(cot_rows)[:, 0, :]
    padded = jnp.pad(window, ((TAPS - 1, 0), (0, 0), (0, 0)))
    short_out = jnp.zeros((window_len, 3, channels), jnp.float32)
    for tap_index in range(TAPS):
        piece = padded[TAPS - 1 - tap_index : TAPS - 1 - tap_index + window_len].astype(jnp.float32)
        short_out = short_out + short_taps[tap_index] * piece
    short_b = short_out.astype(jnp.bfloat16)
    query_f = short_b[:, 0].astype(jnp.float32)
    key_f = short_b[:, 1].astype(jnp.float32)
    value_f = short_b[:, 2].astype(jnp.float32)
    mixed = (key_f * value_f).astype(jnp.bfloat16).astype(jnp.float32)
    grad_f = grad_chan.astype(jnp.float32)
    d_long = grad_f * query_f
    long_part, mixed_part, grad_res = modal_local(mixed, d_long, residue, decay_rate, 128)
    long_out = long_part + skip_gain * mixed
    gated = (query_f * long_out).astype(jnp.bfloat16)
    gated_rows = outbound(gated[:, None, :])
    d_query = grad_f * long_out
    d_mixed = mixed_part + skip_gain * d_long
    grad_gain = jnp.sum(d_long * mixed, axis=0)
    d_short = jnp.stack([d_query, d_mixed * value_f, d_mixed * key_f], axis=1)
    tail = jnp.pad(d_short, ((0, TAPS - 1), (0, 0), (0, 0)))
    d_window = jnp.zeros((window_len, 3, channels), jnp.float32)
    tap_grads = []
    for tap_index in range(TAPS):
        d_window = d_window + short_taps[tap_index] * tail[tap_index : tap_index + window_len]
        piece = padded[TAPS - 1 - tap_index : TAPS - 1 - tap_index + window_len].astype(jnp.float32)
        tap_grads.append(jnp.sum(d_short * piece, axis=0))
    grad_rows = outbound(d_window.astype(jnp.bfloat16))
    return (
        gated_rows.reshape(1, 1, capacity, model_width),
        grad_rows.reshape(1, 1, capacity, 3 * model_width),
        jnp.stack(tap_grads, axis=0),
        grad_res,
        grad_gain,
    )


def per_device(features, counts, short_taps, residue, decay_rate, skip_gain, cotangent):
    results = moved_operator(
        features, counts, short_taps, residue, decay_rate, skip_gain, cotangent
    )
    grad_tap, grad_res, grad_gain = lax.psum((results[2], results[3], results[4]), "dp")
    return (results[0], results[1], grad_tap, grad_res, grad_gain)


def solution(mesh):
    in_specs = (
        P("dp", "ctx", None, None),
        P("dp", "ctx"),
        P(None, None, "ctx"),
        P(None, "ctx"),
        P(None, "ctx"),
        P("ctx"),
        P("dp", "ctx", None, None),
    )
    out_specs = (
        P("dp", "ctx", None, None),
        P("dp", "ctx", None, None),
        P(None, None, "ctx"),
        P(None, "ctx"),
        P("ctx"),
    )
    return jax.shard_map(
        per_device, mesh=mesh, in_specs=in_specs, out_specs=out_specs, check_vma=False
    )
```

profile of v0, /device:TPU:0, one launch (start us, length us, event | category | flops | bytes accessed | tf_op | source)
XLA Modules:
  0.0 809.7 jit_solution(16444914577203407402)
XLA Ops:
  0.6 10.0 %copy.211 = bf16[248,1,4096]{0,1,2:T(2,128)(2,1)} copy(bf16[248,1,4096]{2,0,1:T(8,128)(2,1)} %bitcast.210) | data formatting | bytes 4063232 | tf_op jit(solution)/shard_map/reshape;squeeze | solution.py:71
  11.1 23.6 %reduce.2 = bf16[4096,248]{1,0:T(8,128)(2,1)S(1)} reduce(bf16[4096,1,248]{2,1,0:T(2,128)(2,1)} %bitcast.196, bf16[]{:T(256)} %broadcast.388), dimensions={1}, to_apply=%bitcast.179.reduce_sub_computation | reduce | bytes 4063234
  40.8 7.3 all-to-all-start.2
  48.0 8.4 %copy.192 = bf16[1,1,248,12288]{2,3,1,0:T(8,128)(2,1)} copy(bf16[1,1,248,12288]{3,2,1,0:T(8,128)(2,1)} %param.9) | data formatting | bytes 12189696 | tf_op args[0]
  56.5 10.4 %copy.193 = bf16[248,3,4096]{0,1,2:T(4,128)(2,1)} copy(bf16[248,3,4096]{0,2,1:T(8,128)(2,1)} %bitcast.192) | data formatting | bytes 12189696 | tf_op jit(solution)/shard_map/reshape;squeeze | solution.py:70
  66.9 27.9 %all-to-all-done.2 = bf16[8,2,63488]{2,1,0:T(2,128)(2,1)S(1)} async-done(((bf16[8,2,63488]{2,1,0:T(2,128)(2,1)}), bf16[8,2,63488]{2,1,0:T(2,128)(2,1)S(1)}, u32[]{:S(2)}, u32[]{:S(2)}) %all-to-all-start.2) | async-done | bytes 2031648 | tf_op jit(solution)/shard_map/all_to_all | solution.py:88
  101.8 180.8 %all-reduce.2 = s32[8]{0:T(128)S(1)} all-reduce(s32[8]{0:T(128)S(1)} %bitcast_dynamic-update-slice_fusion), channel_id=1, replica_groups=mesh['dp'=4,'ctx'=8] {'ctx'}, use_global_device_ids=true, to_apply=%add.2 | all-reduce | flops 8 | bytes 64 | tf_op jit(solution)/shard_map/lt | solution.py:82
  283.7 54.4 %gather_fusion.1 = f32[16384,32]{1,0:T(8,128)} fusion(f32[32,128]{0,1:T(8,128)S(1)} %copy.201, s32[16384]{0:T(1024)S(1)} %fusion.91), kind=kCustom, calls=%fused_computation.1 | custom fusion | bytes 4259840 | tf_op jit(solution)/shard_map/jit(_take)/gather | solution.py:24
  338.2 6.5 copy.202
  345.2 8.7 %reshape.460 = bf16[4096,1,248]{2,1,0:T(2,128)(2,1)} reshape(bf16[8,2,63488]{2,1,0:T(2,128)(2,1)S(1)} %all-to-all-done.2) | data formatting | bytes 4063232
  366.9 13.0 %copy.239 = bf16[248,3,8,512]{3,0,2,1:T(8,128)(2,1)} copy(bf16[248,3,8,512]{0,1,3,2:T(4,128)(2,1)} %bitcast.6) | data formatting | bytes 12189696 | tf_op jit(solution)/shard_map/all_to_all | solution.py:88
  379.9 23.3 %copy.196 = bf16[1984,3,512]{2,1,0:T(4,128)(2,1)} copy(bf16[1984,3,512]{2,0,1:T(8,128)(2,1)} %bitcast.193) | data formatting | bytes 12189696 | tf_op jit(solution)/shard_map/all_to_all | solution.py:88
  403.2 14.0 %gather_fusion = bf16[1024,3,512]{2,1,0:T(4,128)(2,1)} fusion(bf16[1984,3,512]{2,1,0:T(4,128)(2,1)} %copy.196, s32[1024]{0:T(1024)S(1)} %broadcast_clamp_fusion), kind=kCustom, calls=%fused_computation | custom fusion | bytes 6295552 | tf_op jit(solution)/shard_map/jit(_take)/gather | solution.py:85
  497.1 9.2 %gather_fusion.2 = bf16[1984,512]{1,0:T(8,128)(2,1)} fusion(bf16[1024,512]{1,0:T(8,128)(2,1)S(1)} %get-tuple-element.108, s32[2048]{0:T(1024)S(1)} %pad_clamp_fusion), kind=kCustom, calls=%fused_computation.2 | custom fusion | bytes 4071168 | tf_op jit(solution)/shard_map/jit(_take)/gather | solution.py:91
  524.7 13.9 %fusion.18 = (f32[3,512]{1,0:T(4,128)S(1)}, f32[3,512]{1,0:T(4,128)S(1)}, f32[3,512]{1,0:T(4,128)S(1)}, f32[3,512]{1,0:T(4,128)S(1)}, f32[3,512]{1,0:T(4,128)S(1...) fusion(bf16[1024,3,512]{2,0,1:T(8,128)(2,1)} %copy-done.3, ...), kind=kLoop, calls=%fused_computation.40 | loop fusion | flops 36165120 | bytes 15771648 | tf_op jit(solution)/shard_map/reduce_sum | solution.py:123
  548.6 23.4 %gather_fusion.4 = bf16[1984,3,512]{2,1,0:T(4,128)(2,1)} fusion(bf16[1024,3,512]{2,1,0:T(4,128)(2,1)} %copy.222, s32[2048]{0:T(1024)S(1)} %pad_clamp_fusion), kind=kCustom, calls=%fused_computation.4 | custom fusion | bytes 12197632 | tf_op jit(solution)/shard_map/jit(_take)/gather | solution.py:91
  571.9 16.4 %fusion.25 = f32[16,32]{0,1:T(8,128)S(1)} fusion(f32[16,32,8,16]{3,2,1,0:T(8,128)} %bitcast.195, f32[8,128,32,16]{1,0,3,2:T(8,128)S(1)} %convert_multiply_fusion.20, f32[128]{0:T(128)S(1)} %iota_add_fusion, f32[16,32]{0,1:T(8,128)S(1)} %copy.200), kind=kOutput, calls=%fused_computation.59 | convolution fusion | flops 100859392 | bytes 2363904 | tf_op jit(solution)/shard_map/iagq,rga,irgq->rg/dot_general | solution.py:58
  592.7 11.9 %select_select_fusion = bf16[1984,3,512]{2,1,0:T(4,128)(2,1)} fusion(bf16[1984,3,512]{2,1,0:T(4,128)(2,1)S(1)} %copy-done.2, pred[1984]{0:T(1024)(128)(4,1)S(1)} %compare_and_fusion, pred[1984]{0:T(1024)(128)(4,1)S(1)} %lt.99), kind=kLoop, calls=%fused_computation.12 | loop fusion | flops 6094848 | bytes 12193664 | tf_op jit(solution)/shard_map/jit(_where)/select_n | solution.py:92
  610.4 11.9 %while.11 = (s32[]{:T(128)}, f32[16,32]{1,0:T(8,128)S(1)}, f32[16,32]{1,0:T(8,128)S(1)}, f32[32,128,128]{2,1,0:T(8,128)S(1)}, s32[]{:T(128)}, /*index=5*/s32[]{:T(128)}) while((s32[]{:T(128)}, f32[16,32]{1,0:T(8,128)S(1)}, f32[16,32]{1,0:T(8,128)S(1)}, f32[32,128,128]{2,1,0:T(8,128)S(1)}, s32[]{:T(128)}, ...), condition=%wide.region_14.15_spmd.clone, body=%wide.region_12.14_spmd.clone.sunk | while | flops 2179074 | bytes 2261845 | solution.py:57
  622.5 12.5 %all-reduce.3 = (f32[7,3,512]{2,1,0:T(4,128)S(1)}, f32[16,32]{1,0:T(8,128)}, f32[512]{0:T(512)}) all-reduce(f32[7,3,512]{2,1,0:T(4,128)S(1)} %constant_dynamic-update-slice_fusion, f32[16,32]{1,0:T(8,128)S(1)} %add.246, f32[512]{0:T(512)S(1)} %get-tuple-element.99), channel_id=1, replica_groups=mesh['dp'=4,'ctx'=8] {'dp'}, use_global_device_ids=true, to_apply=%region_11.12 | all-reduce | flops 11776 | bytes 94208 | tf_op jit(solution)/shard_map/psum | solution.py:138
  635.6 6.8 reshape.458
  648.0 139.0 %all-to-all-done.3 = bf16[1984,3,512]{2,1,0:T(4,128)(2,1)} async-done(((bf16[1984,3,512]{2,1,0:T(4,128)(2,1)}), bf16[1984,3,512]{2,1,0:T(4,128)(2,1)}, u32[]{:S(2)}, u32[]{:S(2)}) %all-to-all-start.3) | async-done | bytes 6094880 | tf_op jit(solution)/shard_map/all_to_all | solution.py:93
  787.0 12.5 %copy.223 = bf16[248,3,8,512]{3,2,1,0:T(8,128)(2,1)} copy(bf16[248,3,8,512]{3,1,0,2:T(4,128)(2,1)} %bitcast.43) | data formatting | bytes 12189696 | tf_op jit(solution)/shard_map/all_to_all | solution.py:93
  799.6 9.8 %reshape.389 = bf16[1,1,248,12288]{3,2,1,0:T(8,128)(2,1)} reshape(bf16[248,3,8,512]{3,2,1,0:T(8,128)(2,1)} %copy.223) | data formatting | bytes 12189696 | tf_op jit(solution)/shard_map/reshape | solution.py:127
  (209 shorter events, 163.3 us)
Async XLA Ops:
  40.8 54.1 %all-to-all-start.2 = ((bf16[8,2,63488]{2,1,0:T(2,128)(2,1)}), bf16[8,2,63488]{2,1,0:T(2,128)(2,1)S(1)}, u32[]{:S(2)}, u32[]{:S(2)}) async-start(bf16[8,2,63488]{2,1,0:T(2,128)(2,1)} %reshape.459), calls=%async_computation.2 | async-start | bytes 4063232 | tf_op jit(solution)/shard_map/all_to_all | solution.py:88
  66.9 33.7 %copy-start.16 = (u32[32]{0:T(128)S(1)}, u32[32]{0:T(128)}, u32[]{:S(2)}) copy-start(u32[32]{0:T(128)} %constant.117) | copy-start | bytes 388
  66.9 216.2 %copy-start.12 = (f32[7,3,512]{2,0,1:T(8,128)S(1)}, f32[7,3,512]{2,0,1:T(8,128)}, u32[]{:S(2)}) copy-start(f32[7,3,512]{2,0,1:T(8,128)} %param.11) | copy-start | bytes 129028
  66.9 216.3 %copy-start.14 = (f32[16,32]{1,0:T(8,128)S(1)}, f32[16,32]{1,0:T(8,128)}, u32[]{:S(2)}) copy-start(f32[16,32]{1,0:T(8,128)} %param.13) | copy-start | bytes 6148
  66.9 216.4 %copy-start.13 = (f32[16,32]{1,0:T(8,128)S(1)}, f32[16,32]{1,0:T(8,128)}, u32[]{:S(2)}) copy-start(f32[16,32]{1,0:T(8,128)} %param.12) | copy-start | bytes 6148
  94.9 272.1 %all-to-all-start = ((bf16[248,3,4096]{0,1,2:T(4,128)(2,1)}), bf16[248,3,4096]{0,1,2:T(4,128)(2,1)}, u32[]{:S(2)}, u32[]{:S(2)}) async-start(bf16[248,3,4096]{0,1,2:T(4,128)(2,1)} %copy.193), calls=%async_computation | async-start | bytes 16777216 | tf_op jit(solution)/shard_map/all_to_all | solution.py:88
  365.1 60.9 %copy-start.6 = (bf16[1024,512]{1,0:T(8,128)(2,1)}, bf16[1024,512]{1,0:T(8,128)(2,1)S(1)}, u32[]{:S(2)}) copy-start(bf16[1024,512]{1,0:T(8,128)(2,1)S(1)} %gather_fusion.3) | copy-start | bytes 3145732
  420.3 5.8 copy-start.3
  426.1 1.7 copy-start
  427.7 1.6 copy-start.8
  430.8 27.7 %copy-start.7 = (bf16[64,8,8,128]{3,2,1,0:T(8,128)(2,1)}, bf16[64,8,8,128]{3,2,1,0:T(8,128)(2,1)S(1)}, u32[]{:S(2)}) copy-start(bf16[64,8,8,128]{3,2,1,0:T(8,128)(2,1)S(1)} %copy.250) | copy-start | bytes 3145732
  439.2 2.2 copy-start.10
  446.2 4.4 copy-start.5
  446.3 4.4 copy-start.11
  451.0 120.9 %copy-start.1 = (f32[8,128,32,16]{1,0,3,2:T(8,128)}, f32[8,128,32,16]{1,0,3,2:T(8,128)S(1)}, u32[]{:S(2)}) copy-start(f32[8,128,32,16]{1,0,3,2:T(8,128)S(1)} %convert_multiply_fusion.20) | copy-start | bytes 6291460
  451.0 3.7 copy-start.4
  472.9 5.7 copy-start.9
  488.0 2.9 copy-start.15
  520.3 84.2 %all-to-all-start.1 = ((bf16[8,2,63488]{2,1,0:T(2,128)(2,1)}), bf16[8,2,63488]{2,1,0:T(2,128)(2,1)}, u32[]{:S(2)}, u32[]{:S(2)}) async-start(bf16[8,2,63488]{2,1,0:T(2,128)(2,1)} %reshape.457), calls=%async_computation.1 | async-start | bytes 4063232 | tf_op jit(solution)/shard_map/all_to_all | solution.py:93
  588.4 4.3 copy-start.2
  604.5 182.5 %all-to-all-start.3 = ((bf16[1984,3,512]{2,1,0:T(4,128)(2,1)}), bf16[1984,3,512]{2,1,0:T(4,128)(2,1)}, u32[]{:S(2)}, u32[]{:S(2)}) async-start(bf16[1984,3,512]{2,1,0:T(4,128)(2,1)} %select_select_fusion), calls=%async_computation.3 | async-start | bytes 16252928 | tf_op jit(solution)/shard_map/all_to_all | solution.py:93
where the time goes:
time: 817 us; the launch traced here: 810 us
  local copies, waits for them, and re-layouts  281 us (34%)
  blocking collectives  193 us (24%)
  waiting for transfers between devices  167 us (20%)
  other arithmetic  91 us (11%)
  matrix products  51.8 us (6%)
  starting transfers between devices  22.5 us (3%)
    lt x1, blocking collectives, moved_operator(): back_valid = (slot_ids[None, :] < all_counts[:, None]).reshape(-1)  181 us
    all_to_all x2, waiting for transfers between devices, outbound(): lax.all_to_all(picked, 'ctx', split_axis=0, concat_axis=2, tiled=True)  139 us
    gather x2, local copies, waits for them, and re-layouts, modal_local(): jnp.take(kernel_rows, jnp.clip(lag_grid, 0, row_block - 1), axis=1)  60.9 us
    unnamed x60, local copies, waits for them, and re-layouts  50.1 us
    all_to_all x4, local copies, waits for them, and re-layouts, inbound(): lax.all_to_all(loader_rows, 'ctx', split_axis=2, concat_axis=0, tiled=True)  40.9 us
    gather x2, local copies, waits for them, and re-layouts, outbound(): picked = jnp.take(chan_rows, back_index, axis=0)  32.5 us
    all_to_all x2, waiting for transfers between devices, inbound(): lax.all_to_all(loader_rows, 'ctx', split_axis=2, concat_axis=0, tiled=True)  27.9 us
    unnamed x1, other arithmetic  23.6 us
  transfers between devices with their start and end apart: 4, of which 2 were waited for; matrix products, arithmetic and copies ran while one was open for 26% of the time, Pallas kernels for 0%

commit v1 on v0

v1 whole, which is shorter than its diff:
```python
import functools

import jax
import jax.numpy as jnp
from jax import lax
from jax.experimental import pallas as pl
from jax.experimental.pallas import tpu as pltpu
from jax.sharding import PartitionSpec as P

TAPS = 7
HALO = 8
REACH = TAPS - 1
ROWS = 256
BLK = 128
POLES = 16
GROUP = 16
LANES = 128
PER = LANES // GROUP
F32 = jnp.float32
BF16 = jnp.bfloat16
SKIP_ROW = 3 * TAPS
RES_ROW = SKIP_ROW + 1
DEC_ROW = SKIP_ROW + 2
CNT_ROW = SKIP_ROW + 3
PARAM_ROWS = 32
GRAD_ROWS = 24


def iota(shape, axis):
    return lax.broadcasted_iota(jnp.int32, shape, axis)


def same_filter():
    return (iota((LANES, LANES), 0) // POLES) == (iota((LANES, LANES), 1) // GROUP)


def lane_filter(width):
    return (iota((1, width), 1) % LANES) // GROUP


def column_of(row):
    return jnp.transpose(jnp.broadcast_to(row, (LANES, LANES)))


def fold(full):
    return jnp.sum(full.reshape(PER, POLES, LANES), axis=0)


def unfold(compact):
    return jnp.where(same_filter(), jnp.tile(compact, (PER, 1)), 0.0)


def fill(scratch, rows_bf, left, right, count, capacity):
    own = rows_bf.astype(F32)
    keep = iota((capacity, LANES), 0) < count
    if left is None:
        scratch[0:HALO, :] = jnp.zeros((HALO, LANES), F32)
    else:
        scratch[0:HALO, :] = left.astype(F32)
    scratch[HALO : HALO + capacity, :] = jnp.where(keep, own, 0.0)
    tail_rows = scratch.shape[0] - HALO - capacity
    scratch[HALO + capacity :, :] = jnp.zeros((tail_rows, LANES), F32)
    scratch[pl.ds(HALO + count, HALO), :] = right.astype(F32)


def short_conv(scratch, taps_of):
    total = taps_of(0) * scratch[HALO : HALO + ROWS, :]
    for tap in range(1, TAPS):
        total = total + taps_of(tap) * scratch[HALO - tap : HALO - tap + ROWS, :]
    return total.astype(BF16).astype(F32)


def front(lanes, count, feats, cot, tail, head, cot_head, param, win, grad):
    capacity = cot.shape[0]
    shorts = []
    for m in range(3):
        fill(
            win.at[m], feats[m][:, lanes], tail[m][:, lanes], head[m][:, lanes], count, capacity
        )
        shorts.append(
            short_conv(win.at[m], lambda tap, m=m: param[0, pl.ds(3 * tap + m, 1), lanes])
        )
    fill(grad, cot[:, lanes], None, cot_head[:, lanes], count, capacity)
    query, key, value = shorts
    mixed = (key * value).astype(BF16).astype(F32)
    grad_rows = grad[HALO : HALO + ROWS, :]
    return query, key, value, mixed, grad_rows, grad_rows * query


def state_kernel(groups, sc, fq, fk, fv, cot, tq, tk, tv, hq, hk, hv, hc, param, out, win, grad):
    count = sc[0]

    def group(k, carry):
        lanes = pl.ds(pl.multiple_of(k * LANES, LANES), LANES)
        _, _, _, mixed, _, d_long = front(
            lanes, count, (fq, fk, fv), cot, (tq, tk, tv), (hq, hk, hv), hc, param, win, grad
        )
        dec = column_of(param[0, DEC_ROW : DEC_ROW + 1, lanes])
        dec = jnp.concatenate([dec, dec], axis=1)
        step = iota((LANES, ROWS), 1)
        ahead = count - 1 - step
        powers = jnp.where(ahead >= 0, jnp.exp(-dec * jnp.maximum(ahead, 0).astype(F32)), 0.0)
        after = step - REACH
        inside = jnp.logical_and(after >= 0, after < count)
        back = jnp.where(inside, jnp.exp(-dec * jnp.maximum(after, 0).astype(F32)), 0.0)
        fwd = jnp.dot(powers.astype(BF16), mixed.astype(BF16), preferred_element_type=F32)
        bwd = jnp.dot(back.astype(BF16), d_long.astype(BF16), preferred_element_type=F32)
        same = same_filter()
        out[0:POLES, lanes] = fold(jnp.where(same, fwd, 0.0)).astype(BF16)
        out[POLES : 2 * POLES, lanes] = fold(jnp.where(same, bwd, 0.0)).astype(BF16)
        return carry

    lax.fori_loop(0, groups, group, 0)


def main_kernel(
    groups, shards, sc, fq, fk, fv, cot, tq, tk, tv, hq, hk, hv, hc, param, states,
    out, dfeat, dparam, win, grad, dshort, dwin,
):
    count = sc[0]
    m_step = pl.program_id(1)
    capacity = cot.shape[0]

    def group(k, carry):
        lanes = pl.ds(pl.multiple_of(k * LANES, LANES), LANES)
        query, key, value, mixed, grad_rows, d_long = front(
            lanes, count, (fq, fk, fv), cot, (tq, tk, tv), (hq, hk, hv), hc, param, win, grad
        )
        row = iota((ROWS, LANES), 0)
        reach = row < count + REACH
        own = row < count
        mixed = jnp.where(reach, mixed, 0.0)
        d_long = jnp.where(reach, d_long, 0.0)
        d_own = jnp.where(own, d_long, 0.0)
        same = same_filter()
        res_row = param[0, RES_ROW : RES_ROW + 1, lanes]
        dec_row = param[0, DEC_ROW : DEC_ROW + 1, lanes]
        skip = param[0, SKIP_ROW : SKIP_ROW + 1, lanes]
        res = column_of(res_row)
        dec = column_of(dec_row)
        lane_f = iota((LANES, LANES), 1).astype(F32)
        sub_f = iota((LANES, LANES), 0).astype(F32)

        rate = fold(jnp.where(same, dec, 0.0))
        from_left = jnp.zeros((POLES, LANES), F32)
        from_right = jnp.zeros((POLES, LANES), F32)
        for i in range(shards):
            gap_l = sc[1 + i]
            gap_r = sc[1 + shards + i]
            w_l = jnp.where(gap_l >= 0, jnp.exp(-rate * jnp.maximum(gap_l, 0).astype(F32)), 0.0)
            w_r = jnp.where(gap_r >= 0, jnp.exp(-rate * jnp.maximum(gap_r, 0).astype(F32)), 0.0)
            both = states[i, :, lanes].astype(F32)
            from_left = from_left + w_l * both[0:POLES]
            from_right = from_right + w_r * both[POLES : 2 * POLES]

        pw_lag = jnp.exp(-dec * lane_f)
        turned = (iota((LANES, LANES), 1) * (LANES - 1)) % LANES
        pw_turn = jnp.exp(-dec * turned.astype(F32))
        k_lag = jnp.sum((res * pw_lag).reshape(PER, POLES, LANES), axis=1)
        k_turn = jnp.sum((res * pw_turn).reshape(PER, POLES, LANES), axis=1)
        lower = iota((BLK, BLK), 0) >= iota((BLK, BLK), 1)
        upper = iota((BLK, BLK), 0) <= iota((BLK, BLK), 1)

        def toeplitz(rows, keep):
            parts = []
            for f in range(PER):
                wide = jnp.broadcast_to(rows[f : f + 1, :], (BLK, LANES))
                wide = pltpu.roll(wide, 0, 1, stride=1, stride_axis=0)
                parts.append(jnp.where(keep, wide, 0.0).astype(BF16))
            return jnp.concatenate(parts, axis=1)

        t_fwd = toeplitz(k_turn, lower)
        t_bwd = toeplitz(k_lag, upper)

        def side(x):
            return jnp.concatenate([x[0:BLK], x[BLK:ROWS]], axis=1)

        def stacked(x):
            fil = lane_filter(2 * LANES)
            return jnp.concatenate(
                [jnp.where(fil == f, x, 0.0).astype(BF16) for f in range(PER)], axis=0
            )

        m_side = side(mixed)
        d_side = side(d_long)
        own_side = side(d_own).astype(BF16)
        mirror = iota((BLK, BLK), 0) + iota((BLK, BLK), 1)
        flip = jnp.where(mirror == BLK - 1, 1.0, 0.0).astype(BF16)
        own_flip = jnp.dot(flip, own_side, preferred_element_type=F32).astype(BF16)
        m_stack = stacked(m_side)
        d_stack = stacked(d_side)
        y_fwd = jnp.dot(t_fwd, m_stack, preferred_element_type=F32)
        y_bwd = jnp.dot(t_bwd, d_stack, preferred_element_type=F32)
        pair = lax.dot_general(
            own_flip, m_stack, (((1,), (1,)), ((), ())), preferred_element_type=F32
        )

        pw_rest = jnp.exp(-dec * (BLK - 1.0 - lane_f))
        in_pw = pw_rest.astype(BF16)
        out_pw = jnp.exp(-dec * (lane_f + 1.0)).astype(BF16)
        s_first = jnp.dot(in_pw, mixed[0:BLK].astype(BF16), preferred_element_type=F32)
        carry0 = unfold(from_left)
        carry1 = jnp.exp(-dec * float(BLK)) * carry0 + jnp.where(same, s_first, 0.0)
        carries = jnp.concatenate([carry0, carry1], axis=1)
        out_t = (res_row * jnp.exp(-dec_row * (sub_f + 1.0))).astype(BF16)
        y_fwd = y_fwd + jnp.dot(out_t, carries.astype(BF16), preferred_element_type=F32)
        seen = jnp.dot(out_pw, own_side, preferred_element_type=F32)

        e_second = jnp.dot(out_pw, d_long[BLK:ROWS].astype(BF16), preferred_element_type=F32)
        e_second = jnp.where(same, e_second, 0.0).astype(BF16)
        in_t = (res_row * jnp.exp(-dec_row * (BLK - 1.0 - sub_f))).astype(BF16)
        until = jnp.maximum(count + REACH - row, 0).astype(F32)
        far_t = (res_row * jnp.exp(-dec_row * until)).astype(BF16)
        y_far = jnp.dot(far_t, unfold(from_right).astype(BF16), preferred_element_type=F32)
        y_near = jnp.dot(in_t, e_second, preferred_element_type=F32)

        long_out = jnp.concatenate([y_fwd[:, 0:LANES], y_fwd[:, LANES:]], axis=0) + skip * mixed
        d_mixed = (
            jnp.concatenate([y_bwd[:, 0:LANES] + y_near, y_bwd[:, LANES:]], axis=0)
            + y_far
            + skip * d_long
        )
        gated = jnp.where(own, query * long_out, 0.0)
        out[:, lanes] = gated[0:capacity].astype(BF16)

        lag_rows = []
        for f in range(PER):
            piece = jnp.where(mirror < BLK, pair[:, f * LANES : (f + 1) * LANES], 0.0)
            piece = pltpu.roll(piece, 0, 1, stride=1, stride_axis=0)
            lag_rows.append(jnp.broadcast_to(jnp.sum(piece, axis=0, keepdims=True), (POLES, LANES)))
        lag_sums = jnp.concatenate(lag_rows, axis=0)
        crossed = seen * carries
        res_grad = lag_sums * pw_rest + crossed[:, 0:LANES] + crossed[:, LANES:]
        dparam[RES_ROW : RES_ROW + 1, lanes] = jnp.sum(
            jnp.transpose(res_grad), axis=0, keepdims=True
        )
        dparam[SKIP_ROW : SKIP_ROW + 1, lanes] = jnp.sum(d_own * mixed, axis=0, keepdims=True)

        d_parts = (grad_rows * long_out, d_mixed * value, d_mixed * key)
        for m in range(3):
            d_m = jnp.where(reach, d_parts[m], 0.0)
            dshort[0:ROWS, :] = d_m
            d_m = jnp.where(own, d_m, 0.0)
            total = jnp.zeros((capacity, LANES), F32)
            for tap in range(TAPS):
                weight = param[0, 3 * tap + m : 3 * tap + m + 1, lanes]
                total = total + weight * dshort[tap : tap + capacity, :]
                piece = d_m * win[m, HALO - tap : HALO - tap + ROWS, :]
                dparam[3 * tap + m : 3 * tap + m + 1, lanes] = jnp.sum(
                    piece, axis=0, keepdims=True
                )
            dwin[m, :, lanes] = jnp.where(own[0:capacity], total, 0.0).astype(BF16)
        return carry

    @pl.when(m_step == 0)
    def _():
        dparam[GRAD_ROWS - 1 : GRAD_ROWS, :] = jnp.zeros((1, dparam.shape[1]), F32)
        dshort[ROWS:, :] = jnp.zeros((dshort.shape[0] - ROWS, LANES), F32)
        lax.fori_loop(0, groups, group, 0)

    dfeat[...] = dwin[m_step]


def per_device(features, counts, short_taps, residue, decay_rate, skip_gain, cotangent):
    shards = lax.axis_size("ctx")
    me = lax.axis_index("ctx")
    capacity = features.shape[2]
    width = cotangent.shape[3]
    chan = short_taps.shape[2]
    groups = chan // LANES
    feats = features[0, 0]
    cot = cotangent[0, 0]
    count = counts[0, 0]

    packed = jnp.concatenate(
        [
            short_taps.reshape(3 * TAPS, chan),
            skip_gain.reshape(1, chan),
            residue.T.reshape(1, chan),
            decay_rate.T.reshape(1, chan),
            jnp.broadcast_to(count.astype(F32), (PARAM_ROWS - CNT_ROW, chan)),
        ],
        axis=0,
    )
    params = lax.all_gather(packed, "ctx", axis=0, tiled=False)
    tail = lax.dynamic_slice(feats, (count - HALO, 0), (HALO, 3 * width))
    head = jnp.concatenate([feats[0:HALO], cot[0:HALO]], axis=1)
    tail = lax.ppermute(tail, "ctx", [(i, i + 1) for i in range(shards - 1)])
    head = lax.ppermute(head, "ctx", [(i + 1, i) for i in range(shards - 1)])

    all_counts = params[:, CNT_ROW, 0].astype(jnp.int32)
    ends = jnp.cumsum(all_counts)
    starts = ends - all_counts
    ids = jnp.arange(shards, dtype=jnp.int32)
    gap_l = jnp.where(ids < me, starts[me] - ends, -1)
    gap_r = jnp.where(ids > me, starts - ends[me], -1)
    scalars = jnp.concatenate([count[None], gap_l, gap_r]).astype(jnp.int32)

    def cols(rows, offset):
        return pl.BlockSpec((rows, chan), lambda g, *_: (0, offset * shards + g))

    smem = pl.BlockSpec(memory_space=pltpu.SMEM)
    specs = [smem]
    specs += [cols(capacity, m) for m in range(3)] + [cols(capacity, 0)]
    specs += [cols(HALO, m) for m in range(3)] + [cols(HALO, m) for m in range(4)]
    specs += [pl.BlockSpec((1, PARAM_ROWS, chan), lambda g, *_: (g, 0, 0))]
    args = [scalars, feats, feats, feats, cot, tail, tail, tail, head, head, head, head, params]
    ext = HALO + ROWS + HALO
    states = pl.pallas_call(
        functools.partial(state_kernel, groups),
        grid=(shards,),
        in_specs=specs,
        out_specs=cols(2 * POLES, 0),
        out_shape=jax.ShapeDtypeStruct((2 * POLES, width), BF16),
        scratch_shapes=[pltpu.VMEM((3, ext, LANES), F32), pltpu.VMEM((ext, LANES), F32)],
        name="states",
    )(*args)
    states = lax.all_gather(states, "ctx", axis=0, tiled=False)

    out, dfeat, dparam = pl.pallas_call(
        functools.partial(main_kernel, groups, shards),
        grid=(shards, 3),
        in_specs=specs + [pl.BlockSpec((shards, 2 * POLES, chan), lambda g, *_: (0, 0, g))],
        out_specs=[
            cols(capacity, 0),
            pl.BlockSpec((capacity, chan), lambda g, m: (0, m * shards + g)),
            cols(GRAD_ROWS, 0),
        ],
        out_shape=[
            jax.ShapeDtypeStruct((capacity, width), BF16),
            jax.ShapeDtypeStruct((capacity, 3 * width), BF16),
            jax.ShapeDtypeStruct((GRAD_ROWS, width), F32),
        ],
        scratch_shapes=[
            pltpu.VMEM((3, ext, LANES), F32),
            pltpu.VMEM((ext, LANES), F32),
            pltpu.VMEM((ROWS + HALO, LANES), F32),
            pltpu.VMEM((3, capacity, chan), BF16),
        ],
        name="main",
    )(*args, states)
    grads = lax.psum_scatter(dparam, "ctx", scatter_dimension=1, tiled=True)
    grads = lax.psum(grads, "dp")
    return (
        out[None, None],
        dfeat[None, None],
        grads[0 : 3 * TAPS].reshape(TAPS, 3, chan),
        grads[RES_ROW].reshape(chan // GROUP, POLES).T,
        grads[SKIP_ROW],
    )


def solution(mesh):
    in_specs = (
        P("dp", "ctx", None, None),
        P("dp", "ctx"),
        P(None, None, "ctx"),
        P(None, "ctx"),
        P(None, "ctx"),
        P("ctx"),
        P("dp", "ctx", None, None),
    )
    out_specs = (
        P("dp", "ctx", None, None),
        P("dp", "ctx", None, None),
        P(None, None, "ctx"),
        P(None, "ctx"),
        P("ctx"),
    )
    return jax.shard_map(
        per_device, mesh=mesh, in_specs=in_specs, out_specs=out_specs, check_vma=False
    )
```

time: 817 us -> 282 us (0.35)
  local copies, waits for them, and re-layouts: 281 us -> 9.24 us
  blocking collectives: 193 us -> 44.9 us
  Pallas kernels: 0 us -> 93.1 us
  other arithmetic: 91 us -> 2.33 us
  waiting for transfers between devices: 167 us -> 110 us
  matrix products: 51.8 us -> 0 us
  starting transfers between devices: 22.5 us -> 6.23 us
  between operations: 2.15 us -> 14.8 us
    lt x1 -> x0, blocking collectives: 181 us -> none  [moved_operator(): back_valid = (slot_ids[None, :] < all_counts[:, None]).reshape(-1)]
    all_to_all x4 -> x0, waiting for transfers between devices: 167 us -> none  [the longest x2 139 us: outbound(): lax.all_to_all(picked, 'ctx', split_axis=0, concat_axis=2, tiled=True)]
    gather x7 -> x0, local copies, waits for them, and re-layouts: 112 us -> none  [the longest x2 60.9 us: modal_local(): jnp.take(kernel_rows, jnp.clip(lag_grid, 0, row_block - 1), axis=1)]
    pallas_call x0 -> x2, Pallas kernels: none -> 93.1 us  [the longest x1 73.1 us: per_device(): pl.pallas_call(functools.partial(main_kernel, groups, shards), grid=(shar...]
    reduce_scatter x0 -> x1, waiting for transfers between devices: none -> 60.8 us  [per_device(): grads = lax.psum_scatter(dparam, 'ctx', scatter_dimension=1, tiled=True)]
    all_to_all x6 -> x0, local copies, waits for them, and re-layouts: 54.1 us -> none  [the longest x4 40.9 us: inbound(): lax.all_to_all(loader_rows, 'ctx', split_axis=2, concat_axis=0, tiled=True)]
    dot_general x10 -> x0, matrix products: 51.8 us -> none  [the longest x1 16.4 us: modal_local(): jnp.einsum('iagq,rga,irgq->rg', grad_blocks, out_powers, cross_state, pre...]
    all_gather x0 -> x1, waiting for transfers between devices: none -> 49.3 us  [per_device(): states = lax.all_gather(states, 'ctx', axis=0, tiled=False)]
  transfers between devices with their start and end apart: 4 -> 4, of which waited for: 2 -> 2; matrix products, arithmetic and copies ran while one was open for 26% -> 3% of each run, Pallas kernels for 0% -> 0%
where the time goes in v1:
time: 282 us; the launch traced here: 281 us
  waiting for transfers between devices  110 us (39%)
  Pallas kernels  93.1 us (33%)
  blocking collectives  44.9 us (16%)
  between operations  14.8 us (5%)
  local copies, waits for them, and re-layouts  9.24 us (3%)
  starting transfers between devices  6.23 us (2%)
    pallas_call x1, Pallas kernels, per_device(): pl.pallas_call(functools.partial(main_kernel, groups, shards), grid=(shar...  73.1 us
    reduce_scatter x1, waiting for transfers between devices, per_device(): grads = lax.psum_scatter(dparam, 'ctx', scatter_dimension=1, tiled=True)  60.8 us
    all_gather x1, waiting for transfers between devices, per_device(): states = lax.all_gather(states, 'ctx', axis=0, tiled=False)  49.3 us
    all_gather x1, blocking collectives, per_device(): params = lax.all_gather(packed, 'ctx', axis=0, tiled=False)  33.9 us
    pallas_call x1, Pallas kernels, per_device(): pl.pallas_call(functools.partial(state_kernel, groups), grid=(shards,), i...  19.9 us
    psum x1, blocking collectives, per_device(): grads = lax.psum(grads, 'dp')  11 us
  transfers between devices with their start and end apart: 4, of which 2 were waited for; matrix products, arithmetic and copies ran while one was open for 3% of the time, Pallas kernels for 0%

profile of v1, /device:TPU:0, one launch (start us, length us, event | category | flops | bytes accessed | tf_op | source)
XLA Modules:
  0.0 280.7 jit_solution(16806005599654615592)
XLA Ops:
  7.9 1.2 slice_bitcast_fusion
  9.0 4.9 %collective-permute-start = (bf16[8,12288]{1,0:T(8,128)(2,1)S(1)}, bf16[8,12288]{1,0:T(8,128)(2,1)S(1)}, u32[]{:S(2)}, u32[]{:S(2)}) collective-permute-start(bf16[8,12288]{1,0:T(8,128)(2,1)S(1)} %get-tuple-element.24), channel_id=1, source_target_pairs={{0,1},{1,2},{2,3},{3,4},{4,5},{5,6},{6,7},{8,9},{9,10},{10,11},{11... | collective-permute-start | bytes 589832 | tf_op jit(solution)/shard_map/ppermute | solution.py:288
  13.9 0.8 slice_bitcast_fusion.1
  14.8 1.3 collective-permute-start.1
  16.1 0.8 copy.15
  16.9 0.8 copy.16
  17.8 0.8 copy.14
  18.7 0.7 concatenate.9
  19.4 33.9 %all-gather = f32[256,512]{1,0:T(8,128)S(1)} all-gather(f32[32,512]{1,0:T(8,128)S(1)} %concatenate.9), channel_id=2, replica_groups=mesh['dp'=4,'ctx'=8] {'ctx'}, dimensions={0}, use_global_device_ids=true | all-gather | bytes 589824 | tf_op jit(solution)/shard_map/all_gather | solution.py:285
  53.2 0.2 fusion
  53.7 0.6 constant_dynamic-slice_fusion
  54.2 0.6 compare_select_fusion
  54.9 0.6 dynamic_slice.11
  55.5 0.6 compare_select_fusion.1
  56.1 0.6 pad_add_fusion.sc
  56.8 0.7 copy-done.1
  57.5 19.9 %states.1 = bf16[32,4096]{1,0:T(8,128)(2,1)} custom-call(s32[17]{0:T(128)} %pad_add_fusion.sc, bf16[248,12288]{1,0:T(8,128)(2,1)} %bitcast.32, bf16[248,12288]{1,0:T(8,128)(2,1)} %bitcast.33, bf16[248,12288]{1,0:T(8,128)(2,1)} %bitcast.34, bf16[248,4096]{1,0:T(8,128)(2,1)} %bitcast.38, bf16[8,12288]{1,0:T(8,128)(2,1)} %copy-done.1, ...), custom_call_target="tpu_custom_call" | custom-call | tf_op jit(solution)/shard_map/states/pallas_call | solution.py:309
  77.5 49.3 %all-gather.4.cloned.1.call-done = bf16[256,4096]{1,0:T(8,128)(2,1)} async-done(((bf16[32,4096]{1,0:T(8,128)(2,1)}), bf16[256,4096]{1,0:T(8,128)(2,1)}) %all-gather.4.cloned.1.call-update) | async-done | bytes 2097168 | tf_op jit(solution)/shard_map/all_gather | solution.py:318
  126.8 73.1 %main.1 = (bf16[248,4096]{1,0:T(8,128)(2,1)}, bf16[248,12288]{1,0:T(8,128)(2,1)}, f32[24,4096]{1,0:T(8,128)}) custom-call(s32[17]{0:T(128)} %pad_add_fusion.sc, bf16[248,12288]{1,0:T(8,128)(2,1)} %bitcast.35, bf16[248,12288]{1,0:T(8,128)(2,1)} %bitcast.36, bf16[248,12288]{1,0:T(8,128)(2,1)} %bitcast.37, bf16[248,4096]{1,0:T(8,128)(2,1)} %bitcast.39, ...), custom_call_target="tpu_custom_call" | custom-call | tf_op jit(solution)/shard_map/main/pallas_call | solution.py:320
  200.0 60.8 %reduce-scatter.2.cloned.1.call-done = f32[24,512]{1,0:T(8,128)} async-done(((f32[24,4096]{1,0:T(8,128)}), f32[24,512]{1,0:T(8,128)}) %reduce-scatter.2.cloned.1.call-update) | async-done | bytes 49168 | tf_op jit(solution)/shard_map/reduce_scatter | solution.py:342
  260.8 11.0 %psum.7 = f32[24,512]{1,0:T(8,128)S(1)} all-reduce(f32[24,512]{1,0:T(8,128)} %reduce-scatter.2.cloned.1.call-done), channel_id=1, replica_groups=mesh['dp'=4,'ctx'=8] {'dp'}, use_global_device_ids=true, to_apply=%region_2.3 | all-reduce | flops 12288 | bytes 98304 | tf_op jit(solution)/shard_map/psum | solution.py:343
  271.9 0.6 fusion.1
  272.5 0.7 copy.18
  273.2 0.6 copy.17
  (19 shorter events, 0.7 us)
Async XLA Ops:
  7.2 119.7 %all-gather.4.cloned.1.call-start = ((), (), s32[]{:S(2)}) async-start(), calls=%async_computation.2 | async-start | bytes 2359296 | tf_op jit(solution)/shard_map/all_gather | solution.py:318
  9.0 47.7 %collective-permute-start = (bf16[8,12288]{1,0:T(8,128)(2,1)S(1)}, bf16[8,12288]{1,0:T(8,128)(2,1)S(1)}, u32[]{:S(2)}, u32[]{:S(2)}) collective-permute-start(bf16[8,12288]{1,0:T(8,128)(2,1)S(1)} %get-tuple-element.24), channel_id=1, source_target_pairs={{0,1},{1,2},{2,3},{3,4},{4,5},{5,6},{6,7},{8,9},{9,10},{10,11},{11... | collective-permute-start | bytes 589832 | tf_op jit(solution)/shard_map/ppermute | solution.py:288
  14.8 42.0 %collective-permute-start.1 = (bf16[8,16384]{1,0:T(8,128)(2,1)S(1)}, bf16[8,16384]{1,0:T(8,128)(2,1)S(1)}, u32[]{:S(2)}, u32[]{:S(2)}) collective-permute-start(bf16[8,16384]{1,0:T(8,128)(2,1)S(1)} %pad_maximum_fusion), channel_id=1, source_target_pairs={{1,0},{2,1},{3,2},{4,3},{5,4},{6,5},{7,6},{9,8},{10,9},{11,10},{12... | collective-permute-start | bytes 786440 | tf_op jit(solution)/shard_map/ppermute | solution.py:289
  53.2 3.5 %copy-start.2 = (f32[256,512]{1,0:T(8,128)}, f32[256,512]{1,0:T(8,128)S(1)}, u32[]{:S(2)}) copy-start(f32[256,512]{1,0:T(8,128)S(1)} %all-gather) | copy-start | bytes 1572868
  56.7 0.7 copy-start.1
  56.7 0.8 copy-start
  77.5 183.3 %reduce-scatter.2.cloned.1.call-start = ((), (), s32[]{:S(2)}) async-start(), calls=%async_computation.1 | async-start | bytes 442368 | tf_op jit(solution)/shard_map/reduce_scatter | solution.py:342
Sparse Core Ops, SparseCore 0:
  77.6 49.1 all-gather.3
  200.1 60.6 reduce-scatter.1

commit v2 on v1

--- a/solution.py
+++ b/solution.py
@@ -50,17 +50,18 @@
     return jnp.where(same_filter(), jnp.tile(compact, (PER, 1)), 0.0)
 
 
-def fill(scratch, rows_bf, left, right, count, capacity):
+def fill(scratch, rows_bf, left, right, sc, capacity):
+    count = sc[0]
     own = rows_bf.astype(F32)
     keep = iota((capacity, LANES), 0) < count
     if left is None:
         scratch[0:HALO, :] = jnp.zeros((HALO, LANES), F32)
     else:
-        scratch[0:HALO, :] = left.astype(F32)
+        scratch[0:HALO, :] = jnp.where(sc[1] > 0, left.astype(F32), 0.0)
     scratch[HALO : HALO + capacity, :] = jnp.where(keep, own, 0.0)
     tail_rows = scratch.shape[0] - HALO - capacity
     scratch[HALO + capacity :, :] = jnp.zeros((tail_rows, LANES), F32)
-    scratch[pl.ds(HALO + count, HALO), :] = right.astype(F32)
+    scratch[pl.ds(HALO + count, HALO), :] = jnp.where(sc[2] > 0, right.astype(F32), 0.0)
 
 
 def short_conv(scratch, taps_of):
@@ -70,17 +71,17 @@
     return total.astype(BF16).astype(F32)
 
 
-def front(lanes, count, feats, cot, tail, head, cot_head, param, win, grad):
+def front(lanes, sc, feats, cot, tail, head, cot_head, param, win, grad):
     capacity = cot.shape[0]
     shorts = []
     for m in range(3):
         fill(
-            win.at[m], feats[m][:, lanes], tail[m][:, lanes], head[m][:, lanes], count, capacity
+            win.at[m], feats[m][:, lanes], tail[m][:, lanes], head[m][:, lanes], sc, capacity
         )
         shorts.append(
             short_conv(win.at[m], lambda tap, m=m: param[0, pl.ds(3 * tap + m, 1), lanes])
         )
-    fill(grad, cot[:, lanes], None, cot_head[:, lanes], count, capacity)
+    fill(grad, cot[:, lanes], None, cot_head[:, lanes], sc, capacity)
     query, key, value = shorts
     mixed = (key * value).astype(BF16).astype(F32)
     grad_rows = grad[HALO : HALO + ROWS, :]
@@ -93,7 +94,7 @@
     def group(k, carry):
         lanes = pl.ds(pl.multiple_of(k * LANES, LANES), LANES)
         _, _, _, mixed, _, d_long = front(
-            lanes, count, (fq, fk, fv), cot, (tq, tk, tv), (hq, hk, hv), hc, param, win, grad
+            lanes, sc, (fq, fk, fv), cot, (tq, tk, tv), (hq, hk, hv), hc, param, win, grad
         )
         dec = column_of(param[0, DEC_ROW : DEC_ROW + 1, lanes])
         dec = jnp.concatenate([dec, dec], axis=1)
@@ -106,8 +107,8 @@
         fwd = jnp.dot(powers.astype(BF16), mixed.astype(BF16), preferred_element_type=F32)
         bwd = jnp.dot(back.astype(BF16), d_long.astype(BF16), preferred_element_type=F32)
         same = same_filter()
-        out[0:POLES, lanes] = fold(jnp.where(same, fwd, 0.0)).astype(BF16)
-        out[POLES : 2 * POLES, lanes] = fold(jnp.where(same, bwd, 0.0)).astype(BF16)
+        out[0, :, lanes] = fold(jnp.where(same, fwd, 0.0)).astype(BF16)
+        out[1, :, lanes] = fold(jnp.where(same, bwd, 0.0)).astype(BF16)
         return carry
 
     lax.fori_loop(0, groups, group, 0)
@@ -124,7 +125,7 @@
     def group(k, carry):
         lanes = pl.ds(pl.multiple_of(k * LANES, LANES), LANES)
         query, key, value, mixed, grad_rows, d_long = front(
-            lanes, count, (fq, fk, fv), cot, (tq, tk, tv), (hq, hk, hv), hc, param, win, grad
+            lanes, sc, (fq, fk, fv), cot, (tq, tk, tv), (hq, hk, hv), hc, param, win, grad
         )
         row = iota((ROWS, LANES), 0)
         reach = row < count + REACH
@@ -145,13 +146,13 @@
         from_left = jnp.zeros((POLES, LANES), F32)
         from_right = jnp.zeros((POLES, LANES), F32)
         for i in range(shards):
-            gap_l = sc[1 + i]
-            gap_r = sc[1 + shards + i]
-            w_l = jnp.where(gap_l >= 0, jnp.exp(-rate * jnp.maximum(gap_l, 0).astype(F32)), 0.0)
-            w_r = jnp.where(gap_r >= 0, jnp.exp(-rate * jnp.maximum(gap_r, 0).astype(F32)), 0.0)
-            both = states[i, :, lanes].astype(F32)
-            from_left = from_left + w_l * both[0:POLES]
-            from_right = from_right + w_r * both[POLES : 2 * POLES]
+            gap_l = sc[3 + i]
+            gap_r = sc[3 + shards + i]
+            gap = jnp.maximum(gap_l, gap_r)
+            there = states[i, :, lanes].astype(F32)
+            there = there * jnp.exp(-rate * jnp.maximum(gap, 0).astype(F32))
+            from_left = from_left + jnp.where(gap_l >= 0, there, 0.0)
+            from_right = from_right + jnp.where(gap_r >= 0, there, 0.0)
 
         pw_lag = jnp.exp(-dec * lane_f)
         turned = (iota((LANES, LANES), 1) * (LANES - 1)) % LANES
@@ -261,6 +262,98 @@
     dfeat[...] = dwin[m_step]
 
 
+MESH = pl.DeviceIdType.MESH
+
+
+def meet(peers):
+    barrier = pltpu.get_barrier_semaphore()
+    for peer in peers:
+        pl.semaphore_signal(barrier, inc=1, device_id=peer, device_id_type=MESH)
+    pl.semaphore_wait(barrier, len(peers))
+
+
+def params_kernel(shards, packed, tail, head, params, tail_in, head_in, send, recv, own):
+    dp, me = lax.axis_index("dp"), lax.axis_index("ctx")
+    peers = [(dp, lax.rem(me + d, shards)) for d in range(1, shards)]
+    meet(peers)
+    local = pltpu.make_async_copy(packed, params.at[me], own)
+    local.start()
+    jobs = [(tail, tail_in, peers[0]), (head, head_in, peers[-1])]
+    jobs += [(packed, params.at[me], peer) for peer in peers]
+    copies = []
+    for n, (src, dst, peer) in enumerate(jobs):
+        copies.append(
+            pltpu.make_async_remote_copy(
+                src_ref=src, dst_ref=dst, send_sem=send.at[n], recv_sem=recv.at[n],
+                device_id=peer, device_id_type=MESH,
+            )
+        )
+        copies[-1].start()
+    local.wait()
+    for copy in copies:
+        copy.wait()
+
+
+def spread_kernel(shards, states, seen, send, recv):
+    dp, me = lax.axis_index("dp"), lax.axis_index("ctx")
+    peers = [(dp, lax.rem(me + d, shards)) for d in range(1, shards)]
+    meet(peers)
+    copies = []
+    for n, peer in enumerate(peers):
+        way = (peer[1] < me).astype(jnp.int32)
+        copies.append(
+            pltpu.make_async_remote_copy(
+                src_ref=states.at[way], dst_ref=seen.at[me], send_sem=send.at[n],
+                recv_sem=recv.at[n], device_id=peer, device_id_type=MESH,
+            )
+        )
+        copies[-1].start()
+    for copy in copies:
+        copy.wait()
+
+
+def reduce_kernel(shards, replicas, part, out, by_ctx, by_dp, send, recv, send_dp, recv_dp):
+    dp, me = lax.axis_index("dp"), lax.axis_index("ctx")
+    chan = out.shape[1]
+    peers = [(dp, lax.rem(me + d, shards)) for d in range(1, shards)]
+    others = [(lax.rem(dp + d, replicas), me) for d in range(1, replicas)]
+    meet(peers + others)
+    copies = []
+    for n, peer in enumerate(peers):
+        lanes = pl.ds(pl.multiple_of(peer[1] * chan, LANES), chan)
+        copies.append(
+            pltpu.make_async_remote_copy(
+                src_ref=part.at[:, lanes], dst_ref=by_ctx.at[n], send_sem=send.at[n],
+                recv_sem=recv.at[n], device_id=peer, device_id_type=MESH,
+            )
+        )
+        copies[-1].start()
+    total = part[:, pl.ds(pl.multiple_of(me * chan, LANES), chan)]
+    for n, copy in enumerate(copies):
+        copy.wait()
+        total = total + by_ctx[n]
+    by_dp[dp] = total
+    copies = []
+    for n, peer in enumerate(others):
+        copies.append(
+            pltpu.make_async_remote_copy(
+                src_ref=by_dp.at[dp], dst_ref=by_dp.at[dp], send_sem=send_dp.at[n],
+                recv_sem=recv_dp.at[n], device_id=peer, device_id_type=MESH,
+            )
+        )
+        copies[-1].start()
+    for copy in copies:
+        copy.wait()
+    total = by_dp[0]
+    for n in range(1, replicas):
+        total = total + by_dp[n]
+    out[...] = total
+
+
+def remote(ident):
+    return pltpu.CompilerParams(collective_id=ident, has_side_effects=True)
+
+
 def per_device(features, counts, short_taps, residue, decay_rate, skip_gain, cotangent):
     shards = lax.axis_size("ctx")
     me = lax.axis_index("ctx")
@@ -282,11 +375,26 @@
         ],
         axis=0,
     )
-    params = lax.all_gather(packed, "ctx", axis=0, tiled=False)
     tail = lax.dynamic_slice(feats, (count - HALO, 0), (HALO, 3 * width))
     head = jnp.concatenate([feats[0:HALO], cot[0:HALO]], axis=1)
-    tail = lax.ppermute(tail, "ctx", [(i, i + 1) for i in range(shards - 1)])
-    head = lax.ppermute(head, "ctx", [(i + 1, i) for i in range(shards - 1)])
+    anywhere = pl.BlockSpec(memory_space=pl.ANY)
+    params, tail, head = pl.pallas_call(
+        functools.partial(params_kernel, shards),
+        in_specs=[anywhere] * 3,
+        out_specs=[anywhere] * 3,
+        out_shape=[
+            jax.ShapeDtypeStruct((shards,) + packed.shape, F32),
+            jax.ShapeDtypeStruct(tail.shape, BF16),
+            jax.ShapeDtypeStruct(head.shape, BF16),
+        ],
+        scratch_shapes=[
+            pltpu.SemaphoreType.DMA((shards + 1,)),
+            pltpu.SemaphoreType.DMA((shards + 1,)),
+            pltpu.SemaphoreType.DMA,
+        ],
+        compiler_params=remote(0),
+        name="params",
+    )(packed, tail, head)
 
     all_counts = params[:, CNT_ROW, 0].astype(jnp.int32)
     ends = jnp.cumsum(all_counts)
@@ -294,7 +402,8 @@
     ids = jnp.arange(shards, dtype=jnp.int32)
     gap_l = jnp.where(ids < me, starts[me] - ends, -1)
     gap_r = jnp.where(ids > me, starts - ends[me], -1)
-    scalars = jnp.concatenate([count[None], gap_l, gap_r]).astype(jnp.int32)
+    edges = jnp.stack([me > 0, me < shards - 1]).astype(jnp.int32)
+    scalars = jnp.concatenate([count[None], edges, gap_l, gap_r]).astype(jnp.int32)
 
     def cols(rows, offset):
         return pl.BlockSpec((rows, chan), lambda g, *_: (0, offset * shards + g))
@@ -310,17 +419,28 @@
         functools.partial(state_kernel, groups),
         grid=(shards,),
         in_specs=specs,
-        out_specs=cols(2 * POLES, 0),
-        out_shape=jax.ShapeDtypeStruct((2 * POLES, width), BF16),
+        out_specs=pl.BlockSpec((2, POLES, chan), lambda g: (0, 0, g)),
+        out_shape=jax.ShapeDtypeStruct((2, POLES, width), BF16),
         scratch_shapes=[pltpu.VMEM((3, ext, LANES), F32), pltpu.VMEM((ext, LANES), F32)],
         name="states",
     )(*args)
-    states = lax.all_gather(states, "ctx", axis=0, tiled=False)
+    states = pl.pallas_call(
+        functools.partial(spread_kernel, shards),
+        in_specs=[anywhere],
+        out_specs=anywhere,
+        out_shape=jax.ShapeDtypeStruct((shards, POLES, width), BF16),
+        scratch_shapes=[
+            pltpu.SemaphoreType.DMA((shards - 1,)),
+            pltpu.SemaphoreType.DMA((shards - 1,)),
+        ],
+        compiler_params=remote(1),
+        name="spread",
+    )(states)
 
     out, dfeat, dparam = pl.pallas_call(
         functools.partial(main_kernel, groups, shards),
         grid=(shards, 3),
-        in_specs=specs + [pl.BlockSpec((shards, 2 * POLES, chan), lambda g, *_: (0, 0, g))],
+        in_specs=specs + [pl.BlockSpec((shards, POLES, chan), lambda g, *_: (0, 0, g))],
         out_specs=[
             cols(capacity, 0),
             pl.BlockSpec((capacity, chan), lambda g, m: (0, m * shards + g)),
@@ -339,8 +459,24 @@
         ],
         name="main",
     )(*args, states)
-    grads = lax.psum_scatter(dparam, "ctx", scatter_dimension=1, tiled=True)
-    grads = lax.psum(grads, "dp")
+    replicas = lax.axis_size("dp")
+    vmem = pl.BlockSpec(memory_space=pltpu.VMEM)
+    grads = pl.pallas_call(
+        functools.partial(reduce_kernel, shards, replicas),
+        in_specs=[vmem],
+        out_specs=vmem,
+        out_shape=jax.ShapeDtypeStruct((GRAD_ROWS, chan), F32),
+        scratch_shapes=[
+            pltpu.VMEM((shards - 1, GRAD_ROWS, chan), F32),
+            pltpu.VMEM((replicas, GRAD_ROWS, chan), F32),
+            pltpu.SemaphoreType.DMA((shards - 1,)),
+            pltpu.SemaphoreType.DMA((shards - 1,)),
+            pltpu.SemaphoreType.DMA((replicas - 1,)),
+            pltpu.SemaphoreType.DMA((replicas - 1,)),
+        ],
+        compiler_params=remote(2),
+        name="reduce",
+    )(dparam)
     return (
         out[None, None],
         dfeat[None, None],

time: 282 us -> 179 us (0.63)
  waiting for transfers between devices: 110 us -> 0 us
  Pallas kernels: 93.1 us -> 160 us
  blocking collectives: 44.9 us -> 0 us
  between operations: 14.8 us -> 1.36 us
  starting transfers between devices: 6.23 us -> 0 us
  local copies, waits for them, and re-layouts: 9.24 us -> 12.6 us
    pallas_call x0 -> x3, Pallas kernels: none -> 65.7 us  [the longest x1 22.8 us: per_device(): pl.pallas_call(functools.partial(params_kernel, shards), in_specs=[anywhe...]
    reduce_scatter x1 -> x0, waiting for transfers between devices: 60.8 us -> none  [per_device(): grads = lax.psum_scatter(dparam, 'ctx', scatter_dimension=1, tiled=True)]
    all_gather x1 -> x0, waiting for transfers between devices: 49.3 us -> none  [per_device(): states = lax.all_gather(states, 'ctx', axis=0, tiled=False)]
    all_gather x1 -> x0, blocking collectives: 33.9 us -> none  [per_device(): params = lax.all_gather(packed, 'ctx', axis=0, tiled=False)]
    psum x1 -> x0, blocking collectives: 11 us -> none  [per_device(): grads = lax.psum(grads, 'dp')]
    ppermute x2 -> x0, starting transfers between devices: 6.15 us -> none  [the longest x1 4.85 us: per_device(): tail = lax.ppermute(tail, 'ctx', [(i, i + 1) for i in range(shards - 1)])]
  transfers between devices with their start and end apart: 4 -> 0, of which waited for: 2 -> 0; matrix products, arithmetic and copies ran while one was open for 3% -> 0% of each run, Pallas kernels for 0% -> 0%
where the time goes in v2:
time: 179 us; the launch traced here: 178 us
  Pallas kernels  160 us (89%)
  local copies, waits for them, and re-layouts  12.6 us (7%)
  other arithmetic  3.86 us (2%)
    pallas_call x1, Pallas kernels, per_device(): pl.pallas_call(functools.partial(main_kernel, groups, shards), grid=(shar...  73.9 us
    pallas_call x1, Pallas kernels, per_device(): pl.pallas_call(functools.partial(params_kernel, shards), in_specs=[anywhe...  22.8 us
    pallas_call x1, Pallas kernels, per_device(): pl.pallas_call(functools.partial(reduce_kernel, shards, replicas), in_spe...  21.7 us
    pallas_call x1, Pallas kernels, per_device(): pl.pallas_call(functools.partial(spread_kernel, shards), in_specs=[anywhe...  21.1 us
    pallas_call x1, Pallas kernels, per_device(): pl.pallas_call(functools.partial(state_kernel, groups), grid=(shards,), i...  20.2 us

profile of v2, /device:TPU:0, one launch (start us, length us, event | category | flops | bytes accessed | tf_op | source)
XLA Modules:
  0.0 177.6 jit_solution(9550664746735037325)
XLA Ops:
  1.4 0.8 copy.18
  2.1 0.1 reshape.53
  2.2 0.8 copy.19
  3.1 0.8 copy.17
  3.9 2.5 %concatenate.9.packed = f32[32,512]{1,0:T(8,128)} concatenate(f32[21,512]{1,0:T(8,128)S(1)} %reshape.51, f32[1,512]{1,0:T(1,128)} %bitcast.44, f32[1,512]{1,0:T(1,128)S(1)} %reshape.53, f32[1,512]{1,0:T(1,128)S(1)} %reshape.54, f32[8,512]{1,0:T(8,128)S(1)} %broadcast_in_dim.14), dimensions={0} | concatenate | bytes 131072 | tf_op jit(solution)/shard_map/concatenate | solution.py:368
  6.5 0.8 slice_bitcast_fusion.1
  7.3 1.8 %slice_bitcast_fusion = (bf16[8,12288]{1,0:T(8,128)(2,1)S(1)}, bf16[8,12288]{1,0:T(8,128)(2,1)}) fusion(bf16[1,1,248,12288]{3,2,1,0:T(8,128)(2,1)} %param.7, s32[]{:T(128)S(6)} %select_n.14), kind=kLoop, calls=%fused_computation.1 | loop fusion | bytes 786436 | tf_op jit(solution)/shard_map/slice | solution.py:379
  9.2 0.7 pad_maximum_fusion.head
  9.9 22.8 %params.1 = (f32[8,32,512]{2,1,0:T(8,128)}, bf16[8,12288]{1,0:T(8,128)(2,1)}, bf16[8,16384]{1,0:T(8,128)(2,1)}) custom-call(f32[32,512]{1,0:T(8,128)} %concatenate.9.packed, bf16[8,12288]{1,0:T(8,128)(2,1)} %get-tuple-element.30.tail, bf16[8,16384]{1,0:T(8,128)(2,1)} %pad_maximum_fusion.head), custom_call_target="tpu_custom_call" | custom-call | tf_op jit(solution)/shard_map/params/pallas_call | solution.py:381
  32.7 1.0 convert_reduce_fusion
  33.7 0.2 reduce-window.4
  33.9 0.6 constant_dynamic-slice_fusion
  34.5 0.6 compare_select_fusion
  35.2 0.6 dynamic_slice.13
  35.8 0.6 compare_select_fusion.1
  36.4 0.6 pad_add_fusion.sc
  37.0 20.2 %states.1 = bf16[2,16,4096]{2,1,0:T(8,128)(2,1)} custom-call(s32[19]{0:T(128)} %pad_add_fusion.sc, bf16[248,12288]{1,0:T(8,128)(2,1)} %bitcast.32, bf16[248,12288]{1,0:T(8,128)(2,1)} %bitcast.33, bf16[248,12288]{1,0:T(8,128)(2,1)} %bitcast.34, bf16[248,4096]{1,0:T(8,128)(2,1)} %bitcast.38, bf16[8,12288]{1,0:T(8,128)(2,1)} %get-tuple-element.12.tq.tk.tv, ...), custom_call_target="tpu_custom_call" | custom-call | tf_op jit(solution)/shard_map/states/pallas_call | solution.py:418
  57.2 21.1 %spread.1.states = bf16[8,16,4096]{2,1,0:T(8,128)(2,1)} custom-call(bf16[2,16,4096]{2,1,0:T(8,128)(2,1)} %states.1), custom_call_target="tpu_custom_call" | custom-call | tf_op jit(solution)/shard_map/spread/pallas_call | solution.py:427
  78.3 73.9 %main.1 = (bf16[248,4096]{1,0:T(8,128)(2,1)}, bf16[248,12288]{1,0:T(8,128)(2,1)}, f32[24,4096]{1,0:T(8,128)}) custom-call(s32[19]{0:T(128)} %pad_add_fusion.sc, bf16[248,12288]{1,0:T(8,128)(2,1)} %bitcast.35, bf16[248,12288]{1,0:T(8,128)(2,1)} %bitcast.36, bf16[248,12288]{1,0:T(8,128)(2,1)} %bitcast.37, bf16[248,4096]{1,0:T(8,128)(2,1)} %bitcast.39, ...), custom_call_target="tpu_custom_call" | custom-call | tf_op jit(solution)/shard_map/main/pallas_call | solution.py:440
  152.3 21.7 %reduce.8 = f32[24,512]{1,0:T(8,128)} custom-call(f32[24,4096]{1,0:T(8,128)} %get-tuple-element.16.part), custom_call_target="tpu_custom_call" | custom-call | tf_op jit(solution)/shard_map/reduce/pallas_call | solution.py:464
  174.0 1.4 fusion
  175.5 0.7 copy.21
  176.2 0.8 reshape.56
  177.0 0.6 copy.20
  (5 shorter events, 0.3 us)

commit v3 on v2

--- a/solution.py
+++ b/solution.py
@@ -88,11 +88,12 @@
     return query, key, value, mixed, grad_rows, grad_rows * query
 
 
-def state_kernel(groups, sc, fq, fk, fv, cot, tq, tk, tv, hq, hk, hv, hc, param, out, win, grad):
+def state_kernel(groups, sc, fq, fk, fv, cot, tq, tk, tv, hq, hk, hv, hc, param, out, wins, grad_wins):
     count = sc[0]
 
-    def group(k, carry):
-        lanes = pl.ds(pl.multiple_of(k * LANES, LANES), LANES)
+    def group(k):
+        lanes = pl.ds(k * LANES, LANES)
+        win, grad = wins.at[k], grad_wins.at[k]
         _, _, _, mixed, _, d_long = front(
             lanes, sc, (fq, fk, fv), cot, (tq, tk, tv), (hq, hk, hv), hc, param, win, grad
         )
@@ -109,21 +110,22 @@
         same = same_filter()
         out[0, :, lanes] = fold(jnp.where(same, fwd, 0.0)).astype(BF16)
         out[1, :, lanes] = fold(jnp.where(same, bwd, 0.0)).astype(BF16)
-        return carry
-
-    lax.fori_loop(0, groups, group, 0)
+
+    for k in range(groups):
+        group(k)
 
 
 def main_kernel(
     groups, shards, sc, fq, fk, fv, cot, tq, tk, tv, hq, hk, hv, hc, param, states,
-    out, dfeat, dparam, win, grad, dshort, dwin,
+    out, dfeat, dparam, wins, grad_wins, dshorts, dwin,
 ):
     count = sc[0]
     m_step = pl.program_id(1)
     capacity = cot.shape[0]
 
-    def group(k, carry):
-        lanes = pl.ds(pl.multiple_of(k * LANES, LANES), LANES)
+    def group(k):
+        lanes = pl.ds(k * LANES, LANES)
+        win, grad, dshort = wins.at[k], grad_wins.at[k], dshorts.at[k]
         query, key, value, mixed, grad_rows, d_long = front(
             lanes, sc, (fq, fk, fv), cot, (tq, tk, tv), (hq, hk, hv), hc, param, win, grad
         )
@@ -251,13 +253,13 @@
                     piece, axis=0, keepdims=True
                 )
             dwin[m, :, lanes] = jnp.where(own[0:capacity], total, 0.0).astype(BF16)
-        return carry
 
     @pl.when(m_step == 0)
     def _():
         dparam[GRAD_ROWS - 1 : GRAD_ROWS, :] = jnp.zeros((1, dparam.shape[1]), F32)
-        dshort[ROWS:, :] = jnp.zeros((dshort.shape[0] - ROWS, LANES), F32)
-        lax.fori_loop(0, groups, group, 0)
+        dshorts[:, ROWS:, :] = jnp.zeros((groups, dshorts.shape[1] - ROWS, LANES), F32)
+        for k in range(groups):
+            group(k)
 
     dfeat[...] = dwin[m_step]
 
@@ -421,7 +423,7 @@
         in_specs=specs,
         out_specs=pl.BlockSpec((2, POLES, chan), lambda g: (0, 0, g)),
         out_shape=jax.ShapeDtypeStruct((2, POLES, width), BF16),
-        scratch_shapes=[pltpu.VMEM((3, ext, LANES), F32), pltpu.VMEM((ext, LANES), F32)],
+        scratch_shapes=[pltpu.VMEM((groups, 3, ext, LANES), F32), pltpu.VMEM((groups, ext, LANES), F32)],
         name="states",
     )(*args)
     states = pl.pallas_call(
@@ -452,9 +454,9 @@
             jax.ShapeDtypeStruct((GRAD_ROWS, width), F32),
         ],
         scratch_shapes=[
-            pltpu.VMEM((3, ext, LANES), F32),
-            pltpu.VMEM((ext, LANES), F32),
-            pltpu.VMEM((ROWS + HALO, LANES), F32),
+            pltpu.VMEM((groups, 3, ext, LANES), F32),
+            pltpu.VMEM((groups, ext, LANES), F32),
+            pltpu.VMEM((groups, ROWS + HALO, LANES), F32),
             pltpu.VMEM((3, capacity, chan), BF16),
         ],
         name="main",

time: 179 us -> 179 us (level)
    pallas_call x1, Pallas kernels: 73.9 us -> 76.5 us  [per_device(): pl.pallas_call(functools.partial(main_kernel, groups, shards), grid=(shar...]
where the time goes in v3:
time: 179 us
  Pallas kernels  161 us (90%)
  local copies, waits for them, and re-layouts  12.6 us (7%)
  other arithmetic  3.86 us (2%)
    pallas_call x1, Pallas kernels, per_device(): pl.pallas_call(functools.partial(main_kernel, groups, shards), grid=(shar...  76.5 us
    pallas_call x1, Pallas kernels, per_device(): pl.pallas_call(functools.partial(params_kernel, shards), in_specs=[anywhe...  22.8 us
    pallas_call x1, Pallas kernels, per_device(): pl.pallas_call(functools.partial(reduce_kernel, shards, replicas), in_spe...  21.7 us
    pallas_call x1, Pallas kernels, per_device(): pl.pallas_call(functools.partial(spread_kernel, shards), in_specs=[anywhe...  21.1 us
    pallas_call x1, Pallas kernels, per_device(): pl.pallas_call(functools.partial(state_kernel, groups), grid=(shards,), i...  18.6 us

profile of v3, /device:TPU:0, one launch (start us, length us, event | category | flops | bytes accessed | tf_op | source)
XLA Modules:
  0.0 178.5 jit_solution(256074747918760720)
XLA Ops:
  1.4 0.8 copy.18
  2.1 0.1 reshape.53
  2.2 0.8 copy.19
  3.1 0.8 copy.17
  3.9 2.5 %concatenate.9.packed = f32[32,512]{1,0:T(8,128)} concatenate(f32[21,512]{1,0:T(8,128)S(1)} %reshape.51, f32[1,512]{1,0:T(1,128)} %bitcast.44, f32[1,512]{1,0:T(1,128)S(1)} %reshape.53, f32[1,512]{1,0:T(1,128)S(1)} %reshape.54, f32[8,512]{1,0:T(8,128)S(1)} %broadcast_in_dim.14), dimensions={0} | concatenate | bytes 131072 | tf_op jit(solution)/shard_map/concatenate | solution.py:370
  6.5 0.8 slice_bitcast_fusion.1
  7.3 1.8 %slice_bitcast_fusion = (bf16[8,12288]{1,0:T(8,128)(2,1)S(1)}, bf16[8,12288]{1,0:T(8,128)(2,1)}) fusion(bf16[1,1,248,12288]{3,2,1,0:T(8,128)(2,1)} %param.7, s32[]{:T(128)S(6)} %select_n.14), kind=kLoop, calls=%fused_computation.1 | loop fusion | bytes 786436 | tf_op jit(solution)/shard_map/slice | solution.py:381
  9.2 0.7 pad_maximum_fusion.head
  9.9 22.8 %params.1 = (f32[8,32,512]{2,1,0:T(8,128)}, bf16[8,12288]{1,0:T(8,128)(2,1)}, bf16[8,16384]{1,0:T(8,128)(2,1)}) custom-call(f32[32,512]{1,0:T(8,128)} %concatenate.9.packed, bf16[8,12288]{1,0:T(8,128)(2,1)} %get-tuple-element.30.tail, bf16[8,16384]{1,0:T(8,128)(2,1)} %pad_maximum_fusion.head), custom_call_target="tpu_custom_call" | custom-call | tf_op jit(solution)/shard_map/params/pallas_call | solution.py:383
  32.7 1.0 convert_reduce_fusion
  33.7 0.2 reduce-window.4
  33.9 0.6 constant_dynamic-slice_fusion
  34.5 0.6 compare_select_fusion
  35.2 0.6 dynamic_slice.13
  35.8 0.6 compare_select_fusion.1
  36.4 0.6 pad_add_fusion.sc
  37.0 18.6 %states.1 = bf16[2,16,4096]{2,1,0:T(8,128)(2,1)} custom-call(s32[19]{0:T(128)} %pad_add_fusion.sc, bf16[248,12288]{1,0:T(8,128)(2,1)} %bitcast.32, bf16[248,12288]{1,0:T(8,128)(2,1)} %bitcast.33, bf16[248,12288]{1,0:T(8,128)(2,1)} %bitcast.34, bf16[248,4096]{1,0:T(8,128)(2,1)} %bitcast.38, bf16[8,12288]{1,0:T(8,128)(2,1)} %get-tuple-element.12.tq.tk.tv, ...), custom_call_target="tpu_custom_call" | custom-call | tf_op jit(solution)/shard_map/states/pallas_call | solution.py:420
  55.6 21.1 %spread.1.states = bf16[8,16,4096]{2,1,0:T(8,128)(2,1)} custom-call(bf16[2,16,4096]{2,1,0:T(8,128)(2,1)} %states.1), custom_call_target="tpu_custom_call" | custom-call | tf_op jit(solution)/shard_map/spread/pallas_call | solution.py:429
  76.7 76.5 %main.1 = (bf16[248,4096]{1,0:T(8,128)(2,1)}, bf16[248,12288]{1,0:T(8,128)(2,1)}, f32[24,4096]{1,0:T(8,128)}) custom-call(s32[19]{0:T(128)} %pad_add_fusion.sc, bf16[248,12288]{1,0:T(8,128)(2,1)} %bitcast.35, bf16[248,12288]{1,0:T(8,128)(2,1)} %bitcast.36, bf16[248,12288]{1,0:T(8,128)(2,1)} %bitcast.37, bf16[248,4096]{1,0:T(8,128)(2,1)} %bitcast.39, ...), custom_call_target="tpu_custom_call" | custom-call | tf_op jit(solution)/shard_map/main/pallas_call | solution.py:442
  153.2 21.7 %reduce.8 = f32[24,512]{1,0:T(8,128)} custom-call(f32[24,4096]{1,0:T(8,128)} %get-tuple-element.16.part), custom_call_target="tpu_custom_call" | custom-call | tf_op jit(solution)/shard_map/reduce/pallas_call | solution.py:466
  174.9 1.4 fusion
  176.4 0.7 copy.21
  177.1 0.8 reshape.56
  177.9 0.6 copy.20
  (5 shorter events, 0.3 us)
